TPU v7x, 256 devices: a whole 4x4x8 slice. The times are simulated.
256 devices in a mesh: chain: 64 (over z, y, core), col: 4 (over x).
Axes of the slice: x: 4, y: 4, z: 8, core: 2. Of those that a mesh axis runs over, the one named last changes fastest.
Arguments:
- diagonal_blocks: float32 [192, 256, 256], P('chain', 'col'), may hold values from -2 to 6, as said below
- couplings: float32 [192, 256, 256], P('chain', 'col'), may hold values from -2 to 2
- right_sides: float32 [64, 192, 256], P('col', 'chain'), may hold values from -0.04 to 0.04
Outputs:
- solution: float32 [64, 192, 256], P('col', 'chain')
Inputs may be any that keep to these rules, and one draw needn't show every extreme that they name: `diagonal_blocks`: each block is symmetric, and the block-tridiagonal matrix that the diagonal blocks form with the couplings is positive definite with every eigenvalue 0.0003 or more.
All inputs are finite; a program needn't handle non-finite values.
Results may differ from a plain program's by a relative error of at most 0.0003.
Values sent between devices are 32-bit elements; how exact they have to be, the bound alone decides.
A program may use at most 64 MiB of HBM per device.

v0:
```python
import jax
import jax.numpy as jnp
from jax import lax
from jax.sharding import PartitionSpec as P

finest = lax.Precision.HIGHEST


def passed_along(shard, axis, by):
    size = lax.axis_size(axis)
    pairs = [(i, i + by) for i in range(size) if 0 <= i + by < size]
    return lax.ppermute(shard, axis, pairs)


def matmul(first_factor, second_factor):
    return jnp.dot(first_factor, second_factor, precision=finest)


def invert(matrix):
    lower_factor = jnp.linalg.cholesky(matrix)
    identity = jnp.eye(matrix.shape[0], dtype=matrix.dtype)
    return jax.scipy.linalg.cho_solve((lower_factor, True), identity)


def interior_solve(loads, inverses, products, inner_coups):
    before = jnp.concatenate([jnp.zeros_like(inner_coups), inner_coups], axis=0)

    def interior_forward(solved_prev, entries):
        load_now, coup_prev, inverse_now = entries
        reduced = load_now - matmul(solved_prev, coup_prev)
        solved_now = matmul(reduced, inverse_now.T)
        return (solved_now, solved_now)

    _, solved = lax.scan(interior_forward, jnp.zeros_like(loads[0]), (loads, before, inverses))

    def interior_backward(after, entries):
        solved_now, product = entries
        current = solved_now - matmul(after, product.T)
        return (current, current)

    _, earlier = lax.scan(interior_backward, solved[-1], (solved[:-1], products), reverse=True)
    return jnp.concatenate([earlier, solved[-1:]], axis=0)


def per_device(diagonal_blocks, couplings, right_sides):
    slab_count = diagonal_blocks.shape[0]
    col_width = diagonal_blocks.shape[1]
    inner_count = slab_count - 1
    col_start = lax.axis_index("col") * col_width
    chain_count = lax.axis_size("chain")
    levels = chain_count.bit_length() - 1
    full_diag, full_coup = (
        lax.all_gather(diagonal_blocks[:inner_count], "col", axis=1, tiled=True),
        lax.all_gather(couplings, "col", axis=1, tiled=True),
    )

    def body_forward(inverse_prev, entries):
        diag_now, coup_prev = entries
        product = matmul(inverse_prev, coup_prev)
        inverse_now = invert(diag_now - matmul(coup_prev.T, product))
        return (inverse_now, (inverse_prev, product))

    last_inverse, (early_inverses, products) = lax.scan(
        body_forward, invert(full_diag[0]), (full_diag[1:], full_coup[: inner_count - 1])
    )
    inverses = jnp.concatenate([early_inverses, last_inverse[None]], axis=0)
    inner_coups = full_coup[: inner_count - 1]
    coup_last = full_coup[inner_count - 1]
    coup_sep = full_coup[inner_count]
    last_cols = lax.dynamic_slice_in_dim(coup_last, col_start, col_width, 1)
    tail_start = matmul(last_inverse, last_cols)

    def body_backward(state, entries):
        green_block, tail_block = state
        inverse_now, product = entries
        green_block = inverse_now + matmul(matmul(product, green_block), product.T)
        tail_block = -matmul(product, tail_block)
        return ((green_block, tail_block), None)

    (near_green, near_tail), _ = lax.scan(
        body_backward, (last_inverse, tail_start), (early_inverses, products), reverse=True
    )
    loads = jnp.swapaxes(right_sides, 0, 1)
    interior = interior_solve(loads[:inner_count], inverses, products, inner_coups)
    got_green, got_tail, got_first = passed_along((near_green, near_tail, interior[0]), "chain", -1)
    sep_rows = lax.dynamic_slice_in_dim(coup_sep, col_start, col_width, 0)
    own_block = diagonal_blocks[inner_count].T
    b_part = (
        own_block
        - matmul(coup_last.T, tail_start)
        - matmul(coup_sep, matmul(got_green, sep_rows.T))
    )
    c_part = -matmul(coup_sep, got_tail)
    h_part = (
        loads[inner_count]
        - matmul(interior[inner_count - 1], coup_last)
        - matmul(got_first, coup_sep.T)
    )
    for level_index in range(levels):
        distance = 1 << level_index
        b_full, c_full = (
            lax.all_gather(b_part, "col", axis=1, tiled=True),
            lax.all_gather(c_part, "col", axis=1, tiled=True),
        )
        inverse = invert(b_full)
        coupling_rows = lax.dynamic_slice_in_dim(c_full, col_start, col_width, 0)
        solved_cols = matmul(inverse, c_part)
        solved_loads = matmul(h_part, inverse.T)
        below_blocks, below_loads = passed_along(
            (matmul(c_full.T, solved_cols), matmul(solved_loads, c_full)), "chain", distance
        )
        far_inverse, far_cols, far_loads = passed_along(
            (inverse, solved_cols, solved_loads), "chain", -distance
        )
        b_part = b_part - below_blocks - matmul(c_full, matmul(far_inverse, coupling_rows.T))
        c_part = -matmul(c_full, far_cols)
        h_part = h_part - below_loads - matmul(far_loads, c_full.T)
    b_final = lax.all_gather(b_part, "col", axis=1, tiled=True)
    separator = jax.scipy.linalg.cho_solve((jnp.linalg.cholesky(b_final), True), h_part.T).T
    carried = passed_along(matmul(separator, coup_sep), "chain", 1)
    adjusted = loads[:inner_count]
    adjusted = adjusted.at[0].add(-carried)
    adjusted = adjusted.at[inner_count - 1].add(-matmul(separator, coup_last.T))
    solved_inner = interior_solve(adjusted, inverses, products, inner_coups)
    return jnp.swapaxes(jnp.concatenate([solved_inner, separator[None]], axis=0), 0, 1)


def solution(mesh):
    in_specs = (P("chain", "col", None), P("chain", "col", None), P("col", "chain", None))
    out_specs = P("col", "chain", None)
    return jax.shard_map(
        per_device, mesh=mesh, in_specs=in_specs, out_specs=out_specs, check_vma=False
    )
```

profile of v0, /device:TPU:250, one launch (start us, length us, event | category | flops | bytes accessed | tf_op | source)
XLA Modules:
  0.0 923.8 jit_solution(14875295477138087786)
XLA Ops:
  1.0 13.5 %all_gather.45 = f32[2,256,256]{2,0,1:T(2,128)S(1)} all-gather(f32[2,64,256]{2,0,1:T(2,128)S(1)} %copy.26), channel_id=1, replica_groups=mesh['chain'=64,'col'=4] {'col'}, dimensions={1}, use_global_device_ids=true | all-gather | bytes 655360 | tf_op jit(solution)/shard_map/all_gather | solution.py:53
  37.2 11.7 %cholesky.441 = f32[128,128]{1,0:T(8,128)S(1)} custom-call(f32[128,128]{1,0:T(8,128)S(1)} %convolution_subtract_fusion.24), custom_call_target="Cholesky" | custom-call | tf_op jit(solution)/shard_map/jit(cholesky)/cholesky | solution.py:20
  55.0 19.7 %custom-call.37 = f32[2,128,128]{1,2,0:T(8,128)S(1)} custom-call(f32[2,128,128]{2,1,0:T(8,128)S(1)} %get-tuple-element.218), custom_call_target="InvertDiagBlocksLowerTriangular" | custom-call | tf_op jit(solution)/shard_map/jit(_cho_solve)/triangular_solve | solution.py:22
  77.1 14.0 %all_gather.46 = f32[3,256,256]{2,1,0:T(8,128)S(1)} all-gather(f32[3,64,256]{2,1,0:T(8,128)S(1)} %copy-done.19), channel_id=1, replica_groups=mesh['chain'=64,'col'=4] {'col'}, dimensions={1}, use_global_device_ids=true | all-gather | bytes 983040 | tf_op jit(solution)/shard_map/all_gather | solution.py:54
  115.3 11.7 %cholesky.475 = f32[128,128]{1,0:T(8,128)S(1)} custom-call(f32[128,128]{1,0:T(8,128)S(1)} %convolution_subtract_fusion.23), custom_call_target="Cholesky" | custom-call | tf_op jit(solution)/shard_map/while/body/eval_jaxpr/jit(cholesky)/cholesky | solution.py:20
  133.8 19.7 %custom-call.39 = f32[2,128,128]{1,2,0:T(8,128)S(1)} custom-call(f32[2,128,128]{2,1,0:T(8,128)S(1)} %get-tuple-element.219), custom_call_target="InvertDiagBlocksLowerTriangular" | custom-call | tf_op jit(solution)/shard_map/while/body/eval_jaxpr/jit(_cho_solve)/triangular_solve | solution.py:22
  170.3 12.3 %all_gather.47 = f32[256,256]{0,1:T(8,128)S(1)} all-gather(f32[256,64]{0,1:T(8,128)S(1)} %bitcast.554), channel_id=1, replica_groups=mesh['chain'=64,'col'=4] {'col'}, dimensions={1}, use_global_device_ids=true | all-gather | bytes 327680 | tf_op jit(solution)/shard_map/all_gather | solution.py:103
  185.6 12.7 %all_gather.48 = f32[256,256]{0,1:T(8,128)S(1)} all-gather(f32[256,64]{0,1:T(8,128)S(1)} %fusion.17), channel_id=1, replica_groups=mesh['chain'=64,'col'=4] {'col'}, dimensions={1}, use_global_device_ids=true | all-gather | bytes 327680 | tf_op jit(solution)/shard_map/all_gather | solution.py:102
  220.6 11.7 %cholesky.509 = f32[128,128]{1,0:T(8,128)S(1)} custom-call(f32[128,128]{1,0:T(8,128)S(1)} %convolution_subtract_fusion.22), custom_call_target="Cholesky" | custom-call | tf_op jit(solution)/shard_map/jit(cholesky)/cholesky | solution.py:20
  240.0 19.7 %custom-call.41 = f32[2,128,128]{1,2,0:T(8,128)S(1)} custom-call(f32[2,128,128]{2,1,0:T(8,128)S(1)} %get-tuple-element.220), custom_call_target="InvertDiagBlocksLowerTriangular" | custom-call | tf_op jit(solution)/shard_map/jit(_cho_solve)/triangular_solve | solution.py:22
  276.8 12.2 %all_gather.49 = f32[256,256]{0,1:T(8,128)S(1)} all-gather(f32[256,64]{0,1:T(8,128)S(1)} %convolution_negate_fusion.5), channel_id=1, replica_groups=mesh['chain'=64,'col'=4] {'col'}, dimensions={1}, use_global_device_ids=true | all-gather | bytes 327680 | tf_op jit(solution)/shard_map/all_gather | solution.py:103
  290.3 12.3 %all_gather.50 = f32[256,256]{0,1:T(8,128)S(1)} all-gather(f32[256,64]{0,1:T(8,128)S(1)} %subtract_subtract_fusion.5), channel_id=1, replica_groups=mesh['chain'=64,'col'=4] {'col'}, dimensions={1}, use_global_device_ids=true | all-gather | bytes 327680 | tf_op jit(solution)/shard_map/all_gather | solution.py:102
  344.9 19.7 %custom-call.43 = f32[2,128,128]{1,2,0:T(8,128)S(1)} custom-call(f32[2,128,128]{2,1,0:T(8,128)S(1)} %get-tuple-element.221), custom_call_target="InvertDiagBlocksLowerTriangular" | custom-call | tf_op jit(solution)/shard_map/jit(_cho_solve)/triangular_solve | solution.py:22
  384.7 12.3 %all_gather.51 = f32[256,256]{0,1:T(8,128)S(1)} all-gather(f32[256,64]{0,1:T(8,128)S(1)} %convolution_negate_fusion.4), channel_id=1, replica_groups=mesh['chain'=64,'col'=4] {'col'}, dimensions={1}, use_global_device_ids=true | all-gather | bytes 327680 | tf_op jit(solution)/shard_map/all_gather | solution.py:103
  398.5 12.2 %all_gather.52 = f32[256,256]{0,1:T(8,128)S(1)} all-gather(f32[256,64]{0,1:T(8,128)S(1)} %subtract_subtract_fusion.4), channel_id=1, replica_groups=mesh['chain'=64,'col'=4] {'col'}, dimensions={1}, use_global_device_ids=true | all-gather | bytes 327680 | tf_op jit(solution)/shard_map/all_gather | solution.py:102
  433.0 11.7 %cholesky.577 = f32[128,128]{1,0:T(8,128)S(1)} custom-call(f32[128,128]{1,0:T(8,128)S(1)} %convolution_subtract_fusion.20), custom_call_target="Cholesky" | custom-call | tf_op jit(solution)/shard_map/jit(cholesky)/cholesky | solution.py:20
  451.8 19.7 %custom-call.45 = f32[2,128,128]{1,2,0:T(8,128)S(1)} custom-call(f32[2,128,128]{2,1,0:T(8,128)S(1)} %get-tuple-element.222), custom_call_target="InvertDiagBlocksLowerTriangular" | custom-call | tf_op jit(solution)/shard_map/jit(_cho_solve)/triangular_solve | solution.py:22
  497.7 12.3 %all_gather.53 = f32[256,256]{0,1:T(8,128)S(1)} all-gather(f32[256,64]{0,1:T(8,128)S(1)} %convolution_negate_fusion.3), channel_id=1, replica_groups=mesh['chain'=64,'col'=4] {'col'}, dimensions={1}, use_global_device_ids=true | all-gather | bytes 327680 | tf_op jit(solution)/shard_map/all_gather | solution.py:103
  511.2 12.3 %all_gather.54 = f32[256,256]{0,1:T(8,128)S(1)} all-gather(f32[256,64]{0,1:T(8,128)S(1)} %subtract_subtract_fusion.3), channel_id=1, replica_groups=mesh['chain'=64,'col'=4] {'col'}, dimensions={1}, use_global_device_ids=true | all-gather | bytes 327680 | tf_op jit(solution)/shard_map/all_gather | solution.py:102
  545.7 11.7 %cholesky.611 = f32[128,128]{1,0:T(8,128)S(1)} custom-call(f32[128,128]{1,0:T(8,128)S(1)} %convolution_subtract_fusion.19), custom_call_target="Cholesky" | custom-call | tf_op jit(solution)/shard_map/jit(cholesky)/cholesky | solution.py:20
  565.5 19.7 %custom-call.47 = f32[2,128,128]{1,2,0:T(8,128)S(1)} custom-call(f32[2,128,128]{2,1,0:T(8,128)S(1)} %get-tuple-element.223), custom_call_target="InvertDiagBlocksLowerTriangular" | custom-call | tf_op jit(solution)/shard_map/jit(_cho_solve)/triangular_solve | solution.py:22
  606.4 12.2 %all_gather.55 = f32[256,256]{0,1:T(8,128)S(1)} all-gather(f32[256,64]{0,1:T(8,128)S(1)} %convolution_negate_fusion.2), channel_id=1, replica_groups=mesh['chain'=64,'col'=4] {'col'}, dimensions={1}, use_global_device_ids=true | all-gather | bytes 327680 | tf_op jit(solution)/shard_map/all_gather | solution.py:103
  620.1 12.2 %all_gather.56 = f32[256,256]{0,1:T(8,128)S(1)} all-gather(f32[256,64]{0,1:T(8,128)S(1)} %subtract_subtract_fusion.2), channel_id=1, replica_groups=mesh['chain'=64,'col'=4] {'col'}, dimensions={1}, use_global_device_ids=true | all-gather | bytes 327680 | tf_op jit(solution)/shard_map/all_gather | solution.py:102
  654.6 11.7 %cholesky.645 = f32[128,128]{1,0:T(8,128)S(1)} custom-call(f32[128,128]{1,0:T(8,128)S(1)} %convolution_subtract_fusion.18), custom_call_target="Cholesky" | custom-call | tf_op jit(solution)/shard_map/jit(cholesky)/cholesky | solution.py:20
  673.8 19.7 %custom-call.49 = f32[2,128,128]{1,2,0:T(8,128)S(1)} custom-call(f32[2,128,128]{2,1,0:T(8,128)S(1)} %get-tuple-element.224), custom_call_target="InvertDiagBlocksLowerTriangular" | custom-call | tf_op jit(solution)/shard_map/jit(_cho_solve)/triangular_solve | solution.py:22
  720.7 12.2 %all_gather.57 = f32[256,256]{0,1:T(8,128)S(1)} all-gather(f32[256,64]{0,1:T(8,128)S(1)} %convolution_negate_fusion.1), channel_id=1, replica_groups=mesh['chain'=64,'col'=4] {'col'}, dimensions={1}, use_global_device_ids=true | all-gather | bytes 327680 | tf_op jit(solution)/shard_map/all_gather | solution.py:103
  734.2 12.3 %all_gather.58 = f32[256,256]{0,1:T(8,128)S(1)} all-gather(f32[256,64]{0,1:T(8,128)S(1)} %subtract_subtract_fusion.1), channel_id=1, replica_groups=mesh['chain'=64,'col'=4] {'col'}, dimensions={1}, use_global_device_ids=true | all-gather | bytes 327680 | tf_op jit(solution)/shard_map/all_gather | solution.py:102
  768.7 11.7 %cholesky.679 = f32[128,128]{1,0:T(8,128)S(1)} custom-call(f32[128,128]{1,0:T(8,128)S(1)} %convolution_subtract_fusion.17), custom_call_target="Cholesky" | custom-call | tf_op jit(solution)/shard_map/jit(cholesky)/cholesky | solution.py:20
  789.2 19.7 %custom-call.51 = f32[2,128,128]{1,2,0:T(8,128)S(1)} custom-call(f32[2,128,128]{2,1,0:T(8,128)S(1)} %get-tuple-element.225), custom_call_target="InvertDiagBlocksLowerTriangular" | custom-call | tf_op jit(solution)/shard_map/jit(_cho_solve)/triangular_solve | solution.py:22
  840.2 12.3 %all_gather.59 = f32[256,256]{0,1:T(8,128)S(1)} all-gather(f32[256,64]{0,1:T(8,128)S(1)} %subtract_subtract_fusion), channel_id=1, replica_groups=mesh['chain'=64,'col'=4] {'col'}, dimensions={1}, use_global_device_ids=true | all-gather | bytes 327680 | tf_op jit(solution)/shard_map/all_gather | solution.py:118
  874.7 11.7 %cholesky.713 = f32[128,128]{1,0:T(8,128)S(1)} custom-call(f32[128,128]{1,0:T(8,128)S(1)} %convolution_subtract_fusion.16), custom_call_target="Cholesky" | custom-call | tf_op jit(solution)/shard_map/jit(cholesky)/cholesky | solution.py:119
  893.8 19.7 %custom-call.20 = f32[2,128,128]{1,2,0:T(8,128)S(1)} custom-call(f32[2,128,128]{2,1,0:T(8,128)S(1)} %get-tuple-element.175), custom_call_target="InvertDiagBlocksLowerTriangular" | custom-call | tf_op jit(solution)/shard_map/jit(_cho_solve)/triangular_solve | solution.py:119
  (472 shorter events, 493.2 us)
Async XLA Ops:
  158.3 10.2 %collective-permute-start.19 = (f32[16,256]{1,0:T(8,128)}, f32[16,256]{1,0:T(8,128)S(1)}, u32[]{:S(2)}, u32[]{:S(2)}) collective-permute-start(f32[16,256]{1,0:T(8,128)} %convolution_subtract_fusion.29), channel_id=1, source_target_pairs={{4,0},{8,4},{12,8},{16,12},{20,16},{24,20},{28,24},{32,28},{36,32}... | collective-permute-start | bytes 49160 | tf_op jit(solution)/shard_map/ppermute | solution.py:12
  161.7 20.9 %collective-permute-start = (f32[256,256]{1,0:T(8,128)}, f32[256,256]{1,0:T(8,128)S(1)}, u32[]{:S(2)}, u32[]{:S(2)}) collective-permute-start(f32[256,256]{1,0:T(8,128)} %convolution_add_fusion), channel_id=1, source_target_pairs={{4,0},{8,4},{12,8},{16,12},{20,16},{24,20},{28,24},{32,28},{36,32}... | collective-permute-start | bytes 786440 | tf_op jit(solution)/shard_map/ppermute | solution.py:12
  262.1 13.5 %collective-permute-start.21 = (f32[16,256]{1,0:T(8,128)S(1)}, f32[16,256]{1,0:T(8,128)S(1)}, u32[]{:S(2)}, u32[]{:S(2)}) collective-permute-start(f32[16,256]{1,0:T(8,128)S(1)} %fusion.228), channel_id=1, source_target_pairs={{4,0},{8,4},{12,8},{16,12},{20,16},{24,20},{28,24},{32,28},{36,32}... | collective-permute-start | bytes 49160 | tf_op jit(solution)/shard_map/ppermute | solution.py:12
  265.4 10.4 %collective-permute-start.4 = (f32[256,64]{0,1:T(8,128)S(1)}, f32[256,64]{0,1:T(8,128)S(1)}, u32[]{:S(2)}, u32[]{:S(2)}) collective-permute-start(f32[256,64]{0,1:T(8,128)S(1)} %fusion.229), channel_id=1, source_target_pairs={{4,0},{8,4},{12,8},{16,12},{20,16},{24,20},{28,24},{32,28},{36,32}... | collective-permute-start | bytes 196616 | tf_op jit(solution)/shard_map/ppermute | solution.py:12
  268.1 99.2 %collective-permute-start.20 = (f32[16,256]{1,0:T(8,128)}, f32[16,256]{1,0:T(8,128)S(1)}, u32[]{:S(2)}, u32[]{:S(2)}) collective-permute-start(f32[16,256]{1,0:T(8,128)} %fusion.247), channel_id=1, source_target_pairs={{0,4},{4,8},{8,12},{12,16},{16,20},{20,24},{24,28},{28,32},{32,36}... | collective-permute-start | bytes 49160 | tf_op jit(solution)/shard_map/ppermute | solution.py:12
  270.1 19.0 %collective-permute-start.3 = (f32[256,256]{1,0:T(8,128)S(1)}, f32[256,256]{1,0:T(8,128)S(1)}, u32[]{:S(2)}, u32[]{:S(2)}) collective-permute-start(f32[256,256]{1,0:T(8,128)S(1)} %pad_maximum_fusion.3), channel_id=1, source_target_pairs={{4,0},{8,4},{12,8},{16,12},{20,16},{24,20},{28,24},{32,28},{36,32}... | collective-permute-start | bytes 786440 | tf_op jit(solution)/shard_map/ppermute | solution.py:12
  273.7 15.8 %collective-permute-start.2 = (f32[256,64]{0,1:T(8,128)S(1)}, f32[256,64]{0,1:T(8,128)S(1)}, u32[]{:S(2)}, u32[]{:S(2)}) collective-permute-start(f32[256,64]{0,1:T(8,128)S(1)} %fusion.241), channel_id=1, source_target_pairs={{0,4},{4,8},{8,12},{12,16},{16,20},{20,24},{24,28},{28,32},{32,36}... | collective-permute-start | bytes 196616 | tf_op jit(solution)/shard_map/ppermute | solution.py:12
  367.9 16.2 %collective-permute-start.23 = (f32[16,256]{1,0:T(8,128)S(1)}, f32[16,256]{1,0:T(8,128)S(1)}, u32[]{:S(2)}, u32[]{:S(2)}) collective-permute-start(f32[16,256]{1,0:T(8,128)S(1)} %fusion.209), channel_id=1, source_target_pairs={{8,0},{12,4},{16,8},{20,12},{24,16},{28,20},{32,24},{36,28},{40,32... | collective-permute-start | bytes 49160 | tf_op jit(solution)/shard_map/ppermute | solution.py:12
  370.8 13.4 %collective-permute-start.22 = (f32[16,256]{1,0:T(8,128)S(1)}, f32[16,256]{1,0:T(8,128)S(1)}, u32[]{:S(2)}, u32[]{:S(2)}) collective-permute-start(f32[16,256]{1,0:T(8,128)S(1)} %fusion.249), channel_id=1, source_target_pairs={{0,8},{4,12},{8,16},{12,20},{16,24},{20,28},{24,32},{28,36},{32,40... | collective-permute-start | bytes 49160 | tf_op jit(solution)/shard_map/ppermute | solution.py:12
  372.5 11.9 %collective-permute-start.7 = (f32[256,64]{0,1:T(8,128)S(1)}, f32[256,64]{0,1:T(8,128)S(1)}, u32[]{:S(2)}, u32[]{:S(2)}) collective-permute-start(f32[256,64]{0,1:T(8,128)S(1)} %fusion.227), channel_id=1, source_target_pairs={{8,0},{12,4},{16,8},{20,12},{24,16},{28,20},{32,24},{36,28},{40,32... | collective-permute-start | bytes 196616 | tf_op jit(solution)/shard_map/ppermute | solution.py:12
  378.2 18.8 %collective-permute-start.6 = (f32[256,256]{1,0:T(8,128)S(1)}, f32[256,256]{1,0:T(8,128)S(1)}, u32[]{:S(2)}, u32[]{:S(2)}) collective-permute-start(f32[256,256]{1,0:T(8,128)S(1)} %pad_maximum_fusion.4), channel_id=1, source_target_pairs={{8,0},{12,4},{16,8},{20,12},{24,16},{28,20},{32,24},{36,28},{40,32... | collective-permute-start | bytes 786440 | tf_op jit(solution)/shard_map/ppermute | solution.py:12
  382.9 14.6 %collective-permute-start.5 = (f32[256,64]{0,1:T(8,128)S(1)}, f32[256,64]{0,1:T(8,128)S(1)}, u32[]{:S(2)}, u32[]{:S(2)}) collective-permute-start(f32[256,64]{0,1:T(8,128)S(1)} %fusion.242), channel_id=1, source_target_pairs={{0,8},{4,12},{8,16},{12,20},{16,24},{20,28},{24,32},{28,36},{32,40... | collective-permute-start | bytes 196616 | tf_op jit(solution)/shard_map/ppermute | solution.py:12
  474.5 22.1 %collective-permute-start.25 = (f32[16,256]{1,0:T(8,128)S(1)}, f32[16,256]{1,0:T(8,128)S(1)}, u32[]{:S(2)}, u32[]{:S(2)}) collective-permute-start(f32[16,256]{1,0:T(8,128)S(1)} %fusion.225), channel_id=1, source_target_pairs={{16,0},{20,4},{24,8},{28,12},{32,16},{36,20},{40,24},{44,28},{48,3... | collective-permute-start | bytes 49160 | tf_op jit(solution)/shard_map/ppermute | solution.py:12
  483.0 13.8 %collective-permute-start.10 = (f32[256,64]{0,1:T(8,128)S(1)}, f32[256,64]{0,1:T(8,128)S(1)}, u32[]{:S(2)}, u32[]{:S(2)}) collective-permute-start(f32[256,64]{0,1:T(8,128)S(1)} %fusion.226), channel_id=1, source_target_pairs={{16,0},{20,4},{24,8},{28,12},{32,16},{36,20},{40,24},{44,28},{48,3... | collective-permute-start | bytes 196616 | tf_op jit(solution)/shard_map/ppermute | solution.py:12
  487.9 100.0 %collective-permute-start.24 = (f32[16,256]{1,0:T(8,128)}, f32[16,256]{1,0:T(8,128)S(1)}, u32[]{:S(2)}, u32[]{:S(2)}) collective-permute-start(f32[16,256]{1,0:T(8,128)} %fusion.250), channel_id=1, source_target_pairs={{0,16},{4,20},{8,24},{12,28},{16,32},{20,36},{24,40},{28,44},{32,4... | collective-permute-start | bytes 49160 | tf_op jit(solution)/shard_map/ppermute | solution.py:12
  489.2 20.8 %collective-permute-start.9 = (f32[256,256]{1,0:T(8,128)S(1)}, f32[256,256]{1,0:T(8,128)S(1)}, u32[]{:S(2)}, u32[]{:S(2)}) collective-permute-start(f32[256,256]{1,0:T(8,128)S(1)} %pad_maximum_fusion.5), channel_id=1, source_target_pairs={{16,0},{20,4},{24,8},{28,12},{32,16},{36,20},{40,24},{44,28},{48,3... | collective-permute-start | bytes 786440 | tf_op jit(solution)/shard_map/ppermute | solution.py:12
  495.2 15.2 %collective-permute-start.8 = (f32[256,64]{0,1:T(8,128)S(1)}, f32[256,64]{0,1:T(8,128)S(1)}, u32[]{:S(2)}, u32[]{:S(2)}) collective-permute-start(f32[256,64]{0,1:T(8,128)S(1)} %fusion.243), channel_id=1, source_target_pairs={{0,16},{4,20},{8,24},{12,28},{16,32},{20,36},{24,40},{28,44},{32,4... | collective-permute-start | bytes 196616 | tf_op jit(solution)/shard_map/ppermute | solution.py:12
  588.5 17.3 %collective-permute-start.27 = (f32[16,256]{1,0:T(8,128)S(1)}, f32[16,256]{1,0:T(8,128)S(1)}, u32[]{:S(2)}, u32[]{:S(2)}) collective-permute-start(f32[16,256]{1,0:T(8,128)S(1)} %fusion.210), channel_id=1, source_target_pairs={{32,0},{36,4},{40,8},{44,12},{48,16},{52,20},{56,24},{60,28},{64,3... | collective-permute-start | bytes 49160 | tf_op jit(solution)/shard_map/ppermute | solution.py:12
  594.7 11.2 %collective-permute-start.26 = (f32[16,256]{1,0:T(8,128)S(1)}, f32[16,256]{1,0:T(8,128)S(1)}, u32[]{:S(2)}, u32[]{:S(2)}) collective-permute-start(f32[16,256]{1,0:T(8,128)S(1)} %fusion.252), channel_id=1, source_target_pairs={{0,32},{4,36},{8,40},{12,44},{16,48},{20,52},{24,56},{28,60},{32,6... | collective-permute-start | bytes 49160 | tf_op jit(solution)/shard_map/ppermute | solution.py:12
  596.4 9.7 %collective-permute-start.13 = (f32[256,64]{0,1:T(8,128)S(1)}, f32[256,64]{0,1:T(8,128)S(1)}, u32[]{:S(2)}, u32[]{:S(2)}) collective-permute-start(f32[256,64]{0,1:T(8,128)S(1)} %fusion.224), channel_id=1, source_target_pairs={{32,0},{36,4},{40,8},{44,12},{48,16},{52,20},{56,24},{60,28},{64,3... | collective-permute-start | bytes 196616 | tf_op jit(solution)/shard_map/ppermute | solution.py:12
  601.0 17.7 %collective-permute-start.12 = (f32[256,256]{1,0:T(8,128)S(1)}, f32[256,256]{1,0:T(8,128)S(1)}, u32[]{:S(2)}, u32[]{:S(2)}) collective-permute-start(f32[256,256]{1,0:T(8,128)S(1)} %pad_maximum_fusion.6), channel_id=1, source_target_pairs={{32,0},{36,4},{40,8},{44,12},{48,16},{52,20},{56,24},{60,28},{64,3... | collective-permute-start | bytes 786440 | tf_op jit(solution)/shard_map/ppermute | solution.py:12
  604.5 14.6 %collective-permute-start.11 = (f32[256,64]{0,1:T(8,128)S(1)}, f32[256,64]{0,1:T(8,128)S(1)}, u32[]{:S(2)}, u32[]{:S(2)}) collective-permute-start(f32[256,64]{0,1:T(8,128)S(1)} %fusion.244), channel_id=1, source_target_pairs={{0,32},{4,36},{8,40},{12,44},{16,48},{20,52},{24,56},{28,60},{32,6... | collective-permute-start | bytes 196616 | tf_op jit(solution)/shard_map/ppermute | solution.py:12
  696.5 23.1 %collective-permute-start.29 = (f32[16,256]{1,0:T(8,128)S(1)}, f32[16,256]{1,0:T(8,128)S(1)}, u32[]{:S(2)}, u32[]{:S(2)}) collective-permute-start(f32[16,256]{1,0:T(8,128)S(1)} %fusion.222), channel_id=1, source_target_pairs={{64,0},{68,4},{72,8},{76,12},{80,16},{84,20},{88,24},{92,28},{96,3... | collective-permute-start | bytes 49160 | tf_op jit(solution)/shard_map/ppermute | solution.py:12
  706.9 12.9 %collective-permute-start.16 = (f32[256,64]{0,1:T(8,128)S(1)}, f32[256,64]{0,1:T(8,128)S(1)}, u32[]{:S(2)}, u32[]{:S(2)}) collective-permute-start(f32[256,64]{0,1:T(8,128)S(1)} %fusion.223), channel_id=1, source_target_pairs={{64,0},{68,4},{72,8},{76,12},{80,16},{84,20},{88,24},{92,28},{96,3... | collective-permute-start | bytes 196616 | tf_op jit(solution)/shard_map/ppermute | solution.py:12
  711.5 100.1 %collective-permute-start.28 = (f32[16,256]{1,0:T(8,128)}, f32[16,256]{1,0:T(8,128)S(1)}, u32[]{:S(2)}, u32[]{:S(2)}) collective-permute-start(f32[16,256]{1,0:T(8,128)} %fusion.253), channel_id=1, source_target_pairs={{0,64},{4,68},{8,72},{12,76},{16,80},{20,84},{24,88},{28,92},{32,9... | collective-permute-start | bytes 49160 | tf_op jit(solution)/shard_map/ppermute | solution.py:12
  712.8 20.2 %collective-permute-start.15 = (f32[256,256]{1,0:T(8,128)S(1)}, f32[256,256]{1,0:T(8,128)S(1)}, u32[]{:S(2)}, u32[]{:S(2)}) collective-permute-start(f32[256,256]{1,0:T(8,128)S(1)} %pad_maximum_fusion.7), channel_id=1, source_target_pairs={{64,0},{68,4},{72,8},{76,12},{80,16},{84,20},{88,24},{92,28},{96,3... | collective-permute-start | bytes 786440 | tf_op jit(solution)/shard_map/ppermute | solution.py:12
  718.3 15.2 %collective-permute-start.14 = (f32[256,64]{0,1:T(8,128)S(1)}, f32[256,64]{0,1:T(8,128)S(1)}, u32[]{:S(2)}, u32[]{:S(2)}) collective-permute-start(f32[256,64]{0,1:T(8,128)S(1)} %fusion.245), channel_id=1, source_target_pairs={{0,64},{4,68},{8,72},{12,76},{16,80},{20,84},{24,88},{28,92},{32,9... | collective-permute-start | bytes 196616 | tf_op jit(solution)/shard_map/ppermute | solution.py:12
  811.9 19.1 %collective-permute-start.31 = (f32[16,256]{1,0:T(8,128)S(1)}, f32[16,256]{1,0:T(8,128)S(1)}, u32[]{:S(2)}, u32[]{:S(2)}) collective-permute-start(f32[16,256]{1,0:T(8,128)S(1)} %fusion.211), channel_id=1, source_target_pairs={{128,0},{132,4},{136,8},{140,12},{144,16},{148,20},{152,24},{156,2... | collective-permute-start | bytes 49160 | tf_op jit(solution)/shard_map/ppermute | solution.py:12
  819.5 11.5 %collective-permute-start.30 = (f32[16,256]{1,0:T(8,128)S(1)}, f32[16,256]{1,0:T(8,128)S(1)}, u32[]{:S(2)}, u32[]{:S(2)}) collective-permute-start(f32[16,256]{1,0:T(8,128)S(1)} %fusion.255), channel_id=1, source_target_pairs={{0,128},{4,132},{8,136},{12,140},{16,144},{20,148},{24,152},{28,15... | collective-permute-start | bytes 49160 | tf_op jit(solution)/shard_map/ppermute | solution.py:12
  820.8 12.3 %collective-permute-start.18 = (f32[256,256]{1,0:T(8,128)S(1)}, f32[256,256]{1,0:T(8,128)S(1)}, u32[]{:S(2)}, u32[]{:S(2)}) collective-permute-start(f32[256,256]{1,0:T(8,128)S(1)} %pad_maximum_fusion.8), channel_id=1, source_target_pairs={{128,0},{132,4},{136,8},{140,12},{144,16},{148,20},{152,24},{156,2... | collective-permute-start | bytes 786440 | tf_op jit(solution)/shard_map/ppermute | solution.py:12
  829.7 10.1 %collective-permute-start.17 = (f32[256,64]{0,1:T(8,128)S(1)}, f32[256,64]{0,1:T(8,128)S(1)}, u32[]{:S(2)}, u32[]{:S(2)}) collective-permute-start(f32[256,64]{0,1:T(8,128)S(1)} %fusion.246), channel_id=1, source_target_pairs={{0,128},{4,132},{8,136},{12,140},{16,144},{20,148},{24,152},{28,15... | collective-permute-start | bytes 196616 | tf_op jit(solution)/shard_map/ppermute | solution.py:12
  915.0 5.1 collective-permute-start.32
  (33 other events, 118.1 us)
where the time goes:
time: 934 us; the launch traced here: 924 us
  other arithmetic  490 us (52%)
  blocking collectives  187 us (20%)
  starting transfers between devices  114 us (12%)
  local copies, waits for them, and re-layouts  56.2 us (6%)
  matrix products  47.9 us (5%)
  between operations  13.9 us (1%)
  waiting for transfers between devices  12 us (1%)
    another operation x55, other arithmetic, invert(): lower_factor = jnp.linalg.cholesky(matrix)  276 us
    another operation x23, other arithmetic, invert(): return jax.scipy.linalg.cho_solve((lower_factor, True), identity)  158 us
    ppermute x33, starting transfers between devices, passed_along(): return lax.ppermute(shard, axis, pairs)  114 us
    all_gather x6, blocking collectives, per_device(): lax.all_gather(b_part, 'col', axis=1, tiled=True)  74 us
    all_gather x6, blocking collectives, per_device(): lax.all_gather(c_part, 'col', axis=1, tiled=True)  73.5 us
    another operation x58, local copies, waits for them, and re-layouts, invert(): return jax.scipy.linalg.cho_solve((lower_factor, True), identity)  35.5 us
    another operation x7, other arithmetic, per_device(): jnp.linalg.cholesky(b_final)  34.6 us
    dot_general x71, matrix products, matmul(): return jnp.dot(first_factor, second_factor, precision=finest)  28.7 us
  transfers between devices with their start and end apart: 33, of which 4 were waited for; matrix products, arithmetic and copies ran while one was open for 22% of the time, Pallas kernels for 0%

commit v1 on v0

--- a/solution.py
+++ b/solution.py
@@ -98,8 +98,15 @@
     )
     for level_index in range(levels):
         distance = 1 << level_index
+
+        def meet_core_on_mesh(local_x):
+            return jnp.concatenate(
+                jax.lax.all_to_all(jnp.stack([local_x] * jax.lax.axis_size("col"), 0), "col", 0, 0),
+                axis=1,
+            )
+
         b_full, c_full = (
-            lax.all_gather(b_part, "col", axis=1, tiled=True),
+            meet_core_on_mesh(b_part),
             lax.all_gather(c_part, "col", axis=1, tiled=True),
         )
         inverse = invert(b_full)

time: 934 us -> 906 us (0.970)
  blocking collectives: 187 us -> 114 us
  waiting for transfers between devices: 12 us -> 35.9 us
  starting transfers between devices: 114 us -> 124 us
    all_gather x6 -> x0, blocking collectives: 74 us -> none  [per_device(): lax.all_gather(b_part, 'col', axis=1, tiled=True)]
    all_to_all x0 -> x6, starting transfers between devices: none -> 28.1 us  [meet_core_on_mesh(): jax.lax.all_to_all(jnp.stack([local_x] * jax.lax.axis_size('col'), 0), 'c...]
    ppermute x33, waiting for transfers between devices: 12 us -> 35.9 us  [passed_along(): return lax.ppermute(shard, axis, pairs)]
    ppermute x33, starting transfers between devices: 114 us -> 95.9 us  [passed_along(): return lax.ppermute(shard, axis, pairs)]
  transfers between devices with their start and end apart: 33 -> 39, of which waited for: 4 -> 9; matrix products, arithmetic and copies ran while one was open for 22% -> 24% of each run, Pallas kernels for 0% -> 0%
where the time goes in v1:
time: 906 us; the launch traced here: 890 us
  other arithmetic  491 us (54%)
  starting transfers between devices  124 us (14%)
  blocking collectives  114 us (13%)
  local copies, waits for them, and re-layouts  55.2 us (6%)
  matrix products  53.4 us (6%)
  waiting for transfers between devices  35.9 us (4%)
  between operations  14.4 us (2%)
    another operation x55, other arithmetic, invert(): lower_factor = jnp.linalg.cholesky(matrix)  277 us
    another operation x23, other arithmetic, invert(): return jax.scipy.linalg.cho_solve((lower_factor, True), identity)  158 us
    ppermute x33, starting transfers between devices, passed_along(): return lax.ppermute(shard, axis, pairs)  95.9 us
    all_gather x6, blocking collectives, per_device(): lax.all_gather(c_part, 'col', axis=1, tiled=True)  74.1 us
    another operation x58, local copies, waits for them, and re-layouts, invert(): return jax.scipy.linalg.cho_solve((lower_factor, True), identity)  36.8 us
    ppermute x33, waiting for transfers between devices, passed_along(): return lax.ppermute(shard, axis, pairs)  35.9 us
    another operation x7, other arithmetic, per_device(): jnp.linalg.cholesky(b_final)  34.6 us
    dot_general x71, matrix products, matmul(): return jnp.dot(first_factor, second_factor, precision=finest)  34.2 us
  transfers between devices with their start and end apart: 39, of which 9 were waited for; matrix products, arithmetic and copies ran while one was open for 24% of the time, Pallas kernels for 0%

profile of v1, /device:TPU:250, one launch (start us, length us, event | category | flops | bytes accessed | tf_op | source)
XLA Modules:
  0.0 889.8 jit_solution(3715239526884997599)
XLA Ops:
  1.0 13.5 %all_gather.27 = f32[2,256,256]{2,0,1:T(2,128)S(1)} all-gather(f32[2,64,256]{2,0,1:T(2,128)S(1)} %copy.26), channel_id=1, replica_groups=mesh['chain'=64,'col'=4] {'col'}, dimensions={1}, use_global_device_ids=true | all-gather | bytes 655360 | tf_op jit(solution)/shard_map/all_gather | solution.py:53
  15.1 11.7 %cholesky.424 = f32[128,128]{1,0:T(8,128)S(1)} custom-call(f32[128,128]{1,0:T(8,128)S(1)} %cholesky.726), custom_call_target="Cholesky" | custom-call | tf_op jit(solution)/shard_map/jit(cholesky)/cholesky | solution.py:20
  37.2 11.7 %cholesky.441 = f32[128,128]{1,0:T(8,128)S(1)} custom-call(f32[128,128]{1,0:T(8,128)S(1)} %convolution_subtract_fusion.24), custom_call_target="Cholesky" | custom-call | tf_op jit(solution)/shard_map/jit(cholesky)/cholesky | solution.py:20
  55.1 19.7 %custom-call.37 = f32[2,128,128]{1,2,0:T(8,128)S(1)} custom-call(f32[2,128,128]{2,1,0:T(8,128)S(1)} %get-tuple-element.218), custom_call_target="InvertDiagBlocksLowerTriangular" | custom-call | tf_op jit(solution)/shard_map/jit(_cho_solve)/triangular_solve | solution.py:22
  77.2 14.0 %all_gather.28 = f32[3,256,256]{2,1,0:T(8,128)S(1)} all-gather(f32[3,64,256]{2,1,0:T(8,128)S(1)} %copy-done.13), channel_id=1, replica_groups=mesh['chain'=64,'col'=4] {'col'}, dimensions={1}, use_global_device_ids=true | all-gather | bytes 983040 | tf_op jit(solution)/shard_map/all_gather | solution.py:54
  93.3 11.7 %cholesky.458 = f32[128,128]{1,0:T(8,128)S(1)} custom-call(f32[128,128]{1,0:T(8,128)S(1)} %cholesky.729), custom_call_target="Cholesky" | custom-call | tf_op jit(solution)/shard_map/while/body/eval_jaxpr/jit(cholesky)/cholesky | solution.py:20
  115.4 11.7 %cholesky.475 = f32[128,128]{1,0:T(8,128)S(1)} custom-call(f32[128,128]{1,0:T(8,128)S(1)} %convolution_subtract_fusion.23), custom_call_target="Cholesky" | custom-call | tf_op jit(solution)/shard_map/while/body/eval_jaxpr/jit(cholesky)/cholesky | solution.py:20
  134.1 19.7 %custom-call.39 = f32[2,128,128]{1,2,0:T(8,128)S(1)} custom-call(f32[2,128,128]{2,1,0:T(8,128)S(1)} %get-tuple-element.219), custom_call_target="InvertDiagBlocksLowerTriangular" | custom-call | tf_op jit(solution)/shard_map/while/body/eval_jaxpr/jit(_cho_solve)/triangular_solve | solution.py:22
  175.5 12.8 %all_gather.29 = f32[256,256]{0,1:T(8,128)S(1)} all-gather(f32[256,64]{0,1:T(8,128)S(1)} %bitcast.584), channel_id=1, replica_groups=mesh['chain'=64,'col'=4] {'col'}, dimensions={1}, use_global_device_ids=true | all-gather | bytes 327680 | tf_op jit(solution)/shard_map/all_gather | solution.py:110
  188.5 11.7 %cholesky.492 = f32[128,128]{1,0:T(8,128)S(1)} custom-call(f32[128,128]{1,0:T(8,128)S(1)} %cholesky.732), custom_call_target="Cholesky" | custom-call | tf_op jit(solution)/shard_map/jit(cholesky)/cholesky | solution.py:20
  210.5 11.7 %cholesky.509 = f32[128,128]{1,0:T(8,128)S(1)} custom-call(f32[128,128]{1,0:T(8,128)S(1)} %convolution_subtract_fusion.22), custom_call_target="Cholesky" | custom-call | tf_op jit(solution)/shard_map/jit(cholesky)/cholesky | solution.py:20
  230.1 19.7 %custom-call.41 = f32[2,128,128]{1,2,0:T(8,128)S(1)} custom-call(f32[2,128,128]{2,1,0:T(8,128)S(1)} %get-tuple-element.220), custom_call_target="InvertDiagBlocksLowerTriangular" | custom-call | tf_op jit(solution)/shard_map/jit(_cho_solve)/triangular_solve | solution.py:22
  277.6 12.3 %all_gather.30 = f32[256,256]{0,1:T(8,128)S(1)} all-gather(f32[256,64]{0,1:T(8,128)S(1)} %convolution_negate_fusion.5), channel_id=1, replica_groups=mesh['chain'=64,'col'=4] {'col'}, dimensions={1}, use_global_device_ids=true | all-gather | bytes 327680 | tf_op jit(solution)/shard_map/all_gather | solution.py:110
  290.0 11.7 %cholesky.526 = f32[128,128]{1,0:T(8,128)S(1)} custom-call(f32[128,128]{1,0:T(8,128)S(1)} %cholesky.735), custom_call_target="Cholesky" | custom-call | tf_op jit(solution)/shard_map/jit(cholesky)/cholesky | solution.py:20
  312.1 11.7 %cholesky.543 = f32[128,128]{1,0:T(8,128)S(1)} custom-call(f32[128,128]{1,0:T(8,128)S(1)} %convolution_subtract_fusion.21), custom_call_target="Cholesky" | custom-call | tf_op jit(solution)/shard_map/jit(cholesky)/cholesky | solution.py:20
  332.6 19.7 %custom-call.43 = f32[2,128,128]{1,2,0:T(8,128)S(1)} custom-call(f32[2,128,128]{2,1,0:T(8,128)S(1)} %get-tuple-element.221), custom_call_target="InvertDiagBlocksLowerTriangular" | custom-call | tf_op jit(solution)/shard_map/jit(_cho_solve)/triangular_solve | solution.py:22
  381.4 12.3 %all_gather.31 = f32[256,256]{0,1:T(8,128)S(1)} all-gather(f32[256,64]{0,1:T(8,128)S(1)} %convolution_negate_fusion.4), channel_id=1, replica_groups=mesh['chain'=64,'col'=4] {'col'}, dimensions={1}, use_global_device_ids=true | all-gather | bytes 327680 | tf_op jit(solution)/shard_map/all_gather | solution.py:110
  393.8 11.7 %cholesky.560 = f32[128,128]{1,0:T(8,128)S(1)} custom-call(f32[128,128]{1,0:T(8,128)S(1)} %cholesky.738), custom_call_target="Cholesky" | custom-call | tf_op jit(solution)/shard_map/jit(cholesky)/cholesky | solution.py:20
  415.9 11.7 %cholesky.577 = f32[128,128]{1,0:T(8,128)S(1)} custom-call(f32[128,128]{1,0:T(8,128)S(1)} %convolution_subtract_fusion.20), custom_call_target="Cholesky" | custom-call | tf_op jit(solution)/shard_map/jit(cholesky)/cholesky | solution.py:20
  435.2 19.7 %custom-call.45 = f32[2,128,128]{1,2,0:T(8,128)S(1)} custom-call(f32[2,128,128]{2,1,0:T(8,128)S(1)} %get-tuple-element.222), custom_call_target="InvertDiagBlocksLowerTriangular" | custom-call | tf_op jit(solution)/shard_map/jit(_cho_solve)/triangular_solve | solution.py:22
  491.3 12.3 %all_gather.32 = f32[256,256]{0,1:T(8,128)S(1)} all-gather(f32[256,64]{0,1:T(8,128)S(1)} %convolution_negate_fusion.3), channel_id=1, replica_groups=mesh['chain'=64,'col'=4] {'col'}, dimensions={1}, use_global_device_ids=true | all-gather | bytes 327680 | tf_op jit(solution)/shard_map/all_gather | solution.py:110
  525.8 11.7 %cholesky.611 = f32[128,128]{1,0:T(8,128)S(1)} custom-call(f32[128,128]{1,0:T(8,128)S(1)} %convolution_subtract_fusion.19), custom_call_target="Cholesky" | custom-call | tf_op jit(solution)/shard_map/jit(cholesky)/cholesky | solution.py:20
  546.4 19.7 %custom-call.47 = f32[2,128,128]{1,2,0:T(8,128)S(1)} custom-call(f32[2,128,128]{2,1,0:T(8,128)S(1)} %get-tuple-element.223), custom_call_target="InvertDiagBlocksLowerTriangular" | custom-call | tf_op jit(solution)/shard_map/jit(_cho_solve)/triangular_solve | solution.py:22
  597.5 12.3 %all_gather.33 = f32[256,256]{0,1:T(8,128)S(1)} all-gather(f32[256,64]{0,1:T(8,128)S(1)} %convolution_negate_fusion.2), channel_id=1, replica_groups=mesh['chain'=64,'col'=4] {'col'}, dimensions={1}, use_global_device_ids=true | all-gather | bytes 327680 | tf_op jit(solution)/shard_map/all_gather | solution.py:110
  632.0 11.7 %cholesky.645 = f32[128,128]{1,0:T(8,128)S(1)} custom-call(f32[128,128]{1,0:T(8,128)S(1)} %convolution_subtract_fusion.18), custom_call_target="Cholesky" | custom-call | tf_op jit(solution)/shard_map/jit(cholesky)/cholesky | solution.py:20
  651.3 19.7 %custom-call.49 = f32[2,128,128]{1,2,0:T(8,128)S(1)} custom-call(f32[2,128,128]{2,1,0:T(8,128)S(1)} %get-tuple-element.224), custom_call_target="InvertDiagBlocksLowerTriangular" | custom-call | tf_op jit(solution)/shard_map/jit(_cho_solve)/triangular_solve | solution.py:22
  702.0 12.3 %all_gather.34 = f32[256,256]{0,1:T(8,128)S(1)} all-gather(f32[256,64]{0,1:T(8,128)S(1)} %convolution_negate_fusion.1), channel_id=1, replica_groups=mesh['chain'=64,'col'=4] {'col'}, dimensions={1}, use_global_device_ids=true | all-gather | bytes 327680 | tf_op jit(solution)/shard_map/all_gather | solution.py:110
  736.5 11.7 %cholesky.679 = f32[128,128]{1,0:T(8,128)S(1)} custom-call(f32[128,128]{1,0:T(8,128)S(1)} %convolution_subtract_fusion.17), custom_call_target="Cholesky" | custom-call | tf_op jit(solution)/shard_map/jit(cholesky)/cholesky | solution.py:20
  756.9 19.7 %custom-call.51 = f32[2,128,128]{1,2,0:T(8,128)S(1)} custom-call(f32[2,128,128]{2,1,0:T(8,128)S(1)} %get-tuple-element.225), custom_call_target="InvertDiagBlocksLowerTriangular" | custom-call | tf_op jit(solution)/shard_map/jit(_cho_solve)/triangular_solve | solution.py:22
  806.3 12.3 %all_gather.35 = f32[256,256]{0,1:T(8,128)S(1)} all-gather(f32[256,64]{0,1:T(8,128)S(1)} %subtract_subtract_fusion), channel_id=1, replica_groups=mesh['chain'=64,'col'=4] {'col'}, dimensions={1}, use_global_device_ids=true | all-gather | bytes 327680 | tf_op jit(solution)/shard_map/all_gather | solution.py:125
  840.8 11.7 %cholesky.713 = f32[128,128]{1,0:T(8,128)S(1)} custom-call(f32[128,128]{1,0:T(8,128)S(1)} %convolution_subtract_fusion.16), custom_call_target="Cholesky" | custom-call | tf_op jit(solution)/shard_map/jit(cholesky)/cholesky | solution.py:126
  859.8 19.7 %custom-call.20 = f32[2,128,128]{1,2,0:T(8,128)S(1)} custom-call(f32[2,128,128]{2,1,0:T(8,128)S(1)} %get-tuple-element.175), custom_call_target="InvertDiagBlocksLowerTriangular" | custom-call | tf_op jit(solution)/shard_map/jit(_cho_solve)/triangular_solve | solution.py:126
  (472 shorter events, 463.2 us)
Async XLA Ops:
  157.9 9.5 %collective-permute-start.19 = (f32[16,256]{1,0:T(8,128)S(1)}, f32[16,256]{1,0:T(8,128)S(1)}, u32[]{:S(2)}, u32[]{:S(2)}) collective-permute-start(f32[16,256]{1,0:T(8,128)S(1)} %convolution_subtract_fusion.29), channel_id=1, source_target_pairs={{4,0},{8,4},{12,8},{16,12},{20,16},{24,20},{28,24},{32,28},{36,32}... | collective-permute-start | bytes 49160 | tf_op jit(solution)/shard_map/ppermute | solution.py:12
  165.0 10.2 %collective-permute-start.1 = (f32[256,64]{1,0:T(8,128)S(1)}, f32[256,64]{1,0:T(8,128)S(1)}, u32[]{:S(2)}, u32[]{:S(2)}) collective-permute-start(f32[256,64]{1,0:T(8,128)S(1)} %convolution_negate_fusion), channel_id=1, source_target_pairs={{4,0},{8,4},{12,8},{16,12},{20,16},{24,20},{28,24},{32,28},{36,32}... | collective-permute-start | bytes 196616 | tf_op jit(solution)/shard_map/ppermute | solution.py:12
  170.6 17.6 %all-to-all-start = ((f32[4,256,64]{1,2,0:T(8,128)}), f32[4,256,64]{1,2,0:T(8,128)S(1)}, u32[]{:S(2)}, u32[]{:S(2)}) async-start(f32[4,256,64]{1,2,0:T(8,128)} %stack.12), calls=%async_computation | async-start | bytes 524288 | tf_op jit(solution)/shard_map/all_to_all | solution.py:104
  252.9 13.5 %collective-permute-start.21 = (f32[16,256]{1,0:T(8,128)S(1)}, f32[16,256]{1,0:T(8,128)S(1)}, u32[]{:S(2)}, u32[]{:S(2)}) collective-permute-start(f32[16,256]{1,0:T(8,128)S(1)} %fusion.228), channel_id=1, source_target_pairs={{4,0},{8,4},{12,8},{16,12},{20,16},{24,20},{28,24},{32,28},{36,32}... | collective-permute-start | bytes 49160 | tf_op jit(solution)/shard_map/ppermute | solution.py:12
  254.9 11.8 %collective-permute-start.3 = (f32[256,256]{1,0:T(8,128)S(1)}, f32[256,256]{1,0:T(8,128)S(1)}, u32[]{:S(2)}, u32[]{:S(2)}) collective-permute-start(f32[256,256]{1,0:T(8,128)S(1)} %pad_maximum_fusion.3), channel_id=1, source_target_pairs={{4,0},{8,4},{12,8},{16,12},{20,16},{24,20},{28,24},{32,28},{36,32}... | collective-permute-start | bytes 786440 | tf_op jit(solution)/shard_map/ppermute | solution.py:12
  259.5 16.9 %collective-permute-start.4 = (f32[256,64]{0,1:T(8,128)}, f32[256,64]{0,1:T(8,128)}, u32[]{:S(2)}, u32[]{:S(2)}) collective-permute-start(f32[256,64]{0,1:T(8,128)} %fusion.229), channel_id=1, source_target_pairs={{4,0},{8,4},{12,8},{16,12},{20,16},{24,20},{28,24},{32,28},{36,32}... | collective-permute-start | bytes 196616 | tf_op jit(solution)/shard_map/ppermute | solution.py:12
  261.4 93.6 %collective-permute-start.20 = (f32[16,256]{1,0:T(8,128)}, f32[16,256]{1,0:T(8,128)S(1)}, u32[]{:S(2)}, u32[]{:S(2)}) collective-permute-start(f32[16,256]{1,0:T(8,128)} %fusion.247), channel_id=1, source_target_pairs={{0,4},{4,8},{8,12},{12,16},{16,20},{20,24},{24,28},{28,32},{32,36}... | collective-permute-start | bytes 49160 | tf_op jit(solution)/shard_map/ppermute | solution.py:12
  271.1 18.7 %all-to-all-start.1 = ((f32[4,256,64]{1,2,0:T(8,128)}), f32[4,256,64]{1,2,0:T(8,128)S(1)}, u32[]{:S(2)}, u32[]{:S(2)}) async-start(f32[4,256,64]{1,2,0:T(8,128)} %stack.13), calls=%async_computation.1 | async-start | bytes 524288 | tf_op jit(solution)/shard_map/all_to_all | solution.py:104
  355.7 15.0 %collective-permute-start.23 = (f32[16,256]{1,0:T(8,128)S(1)}, f32[16,256]{1,0:T(8,128)S(1)}, u32[]{:S(2)}, u32[]{:S(2)}) collective-permute-start(f32[16,256]{1,0:T(8,128)S(1)} %fusion.209), channel_id=1, source_target_pairs={{8,0},{12,4},{16,8},{20,12},{24,16},{28,20},{32,24},{36,28},{40,32... | collective-permute-start | bytes 49160 | tf_op jit(solution)/shard_map/ppermute | solution.py:12
  358.4 12.2 %collective-permute-start.22 = (f32[16,256]{1,0:T(8,128)S(1)}, f32[16,256]{1,0:T(8,128)S(1)}, u32[]{:S(2)}, u32[]{:S(2)}) collective-permute-start(f32[16,256]{1,0:T(8,128)S(1)} %fusion.249), channel_id=1, source_target_pairs={{0,8},{4,12},{8,16},{12,20},{16,24},{20,28},{24,32},{28,36},{32,40... | collective-permute-start | bytes 49160 | tf_op jit(solution)/shard_map/ppermute | solution.py:12
  359.7 11.2 %collective-permute-start.6 = (f32[256,256]{1,0:T(8,128)S(1)}, f32[256,256]{1,0:T(8,128)S(1)}, u32[]{:S(2)}, u32[]{:S(2)}) collective-permute-start(f32[256,256]{1,0:T(8,128)S(1)} %pad_maximum_fusion.4), channel_id=1, source_target_pairs={{8,0},{12,4},{16,8},{20,12},{24,16},{28,20},{32,24},{36,28},{40,32... | collective-permute-start | bytes 786440 | tf_op jit(solution)/shard_map/ppermute | solution.py:12
  364.7 16.4 %collective-permute-start.7 = (f32[256,64]{0,1:T(8,128)S(1)}, f32[256,64]{0,1:T(8,128)S(1)}, u32[]{:S(2)}, u32[]{:S(2)}) collective-permute-start(f32[256,64]{0,1:T(8,128)S(1)} %fusion.227), channel_id=1, source_target_pairs={{8,0},{12,4},{16,8},{20,12},{24,16},{28,20},{32,24},{36,28},{40,32... | collective-permute-start | bytes 196616 | tf_op jit(solution)/shard_map/ppermute | solution.py:12
  376.6 17.0 %all-to-all-start.2 = ((f32[4,256,64]{1,2,0:T(8,128)}), f32[4,256,64]{1,2,0:T(8,128)S(1)}, u32[]{:S(2)}, u32[]{:S(2)}) async-start(f32[4,256,64]{1,2,0:T(8,128)} %stack.14), calls=%async_computation.2 | async-start | bytes 524288 | tf_op jit(solution)/shard_map/all_to_all | solution.py:104
  458.0 19.3 %collective-permute-start.25 = (f32[16,256]{1,0:T(8,128)S(1)}, f32[16,256]{1,0:T(8,128)S(1)}, u32[]{:S(2)}, u32[]{:S(2)}) collective-permute-start(f32[16,256]{1,0:T(8,128)S(1)} %fusion.225), channel_id=1, source_target_pairs={{16,0},{20,4},{24,8},{28,12},{32,16},{36,20},{40,24},{44,28},{48,3... | collective-permute-start | bytes 49160 | tf_op jit(solution)/shard_map/ppermute | solution.py:12
  464.1 13.4 %collective-permute-start.9 = (f32[256,256]{1,0:T(8,128)S(1)}, f32[256,256]{1,0:T(8,128)S(1)}, u32[]{:S(2)}, u32[]{:S(2)}) collective-permute-start(f32[256,256]{1,0:T(8,128)S(1)} %pad_maximum_fusion.5), channel_id=1, source_target_pairs={{16,0},{20,4},{24,8},{28,12},{32,16},{36,20},{40,24},{44,28},{48,3... | collective-permute-start | bytes 786440 | tf_op jit(solution)/shard_map/ppermute | solution.py:12
  468.8 21.3 %collective-permute-start.10 = (f32[256,64]{0,1:T(8,128)}, f32[256,64]{0,1:T(8,128)}, u32[]{:S(2)}, u32[]{:S(2)}) collective-permute-start(f32[256,64]{0,1:T(8,128)} %fusion.226), channel_id=1, source_target_pairs={{16,0},{20,4},{24,8},{28,12},{32,16},{36,20},{40,24},{44,28},{48,3... | collective-permute-start | bytes 196616 | tf_op jit(solution)/shard_map/ppermute | solution.py:12
  474.7 94.1 %collective-permute-start.24 = (f32[16,256]{1,0:T(8,128)}, f32[16,256]{1,0:T(8,128)S(1)}, u32[]{:S(2)}, u32[]{:S(2)}) collective-permute-start(f32[16,256]{1,0:T(8,128)} %fusion.250), channel_id=1, source_target_pairs={{0,16},{4,20},{8,24},{12,28},{16,32},{20,36},{24,40},{28,44},{32,4... | collective-permute-start | bytes 49160 | tf_op jit(solution)/shard_map/ppermute | solution.py:12
  485.4 18.2 %all-to-all-start.3 = ((f32[4,256,64]{1,2,0:T(8,128)}), f32[4,256,64]{1,2,0:T(8,128)S(1)}, u32[]{:S(2)}, u32[]{:S(2)}) async-start(f32[4,256,64]{1,2,0:T(8,128)} %stack.15), calls=%async_computation.3 | async-start | bytes 524288 | tf_op jit(solution)/shard_map/all_to_all | solution.py:104
  569.4 17.3 %collective-permute-start.27 = (f32[16,256]{1,0:T(8,128)S(1)}, f32[16,256]{1,0:T(8,128)S(1)}, u32[]{:S(2)}, u32[]{:S(2)}) collective-permute-start(f32[16,256]{1,0:T(8,128)S(1)} %fusion.210), channel_id=1, source_target_pairs={{32,0},{36,4},{40,8},{44,12},{48,16},{52,20},{56,24},{60,28},{64,3... | collective-permute-start | bytes 49160 | tf_op jit(solution)/shard_map/ppermute | solution.py:12
  573.0 13.7 %collective-permute-start.26 = (f32[16,256]{1,0:T(8,128)S(1)}, f32[16,256]{1,0:T(8,128)S(1)}, u32[]{:S(2)}, u32[]{:S(2)}) collective-permute-start(f32[16,256]{1,0:T(8,128)S(1)} %fusion.252), channel_id=1, source_target_pairs={{0,32},{4,36},{8,40},{12,44},{16,48},{20,52},{24,56},{28,60},{32,6... | collective-permute-start | bytes 49160 | tf_op jit(solution)/shard_map/ppermute | solution.py:12
  574.3 12.6 %collective-permute-start.12 = (f32[256,256]{1,0:T(8,128)S(1)}, f32[256,256]{1,0:T(8,128)S(1)}, u32[]{:S(2)}, u32[]{:S(2)}) collective-permute-start(f32[256,256]{1,0:T(8,128)S(1)} %pad_maximum_fusion.6), channel_id=1, source_target_pairs={{32,0},{36,4},{40,8},{44,12},{48,16},{52,20},{56,24},{60,28},{64,3... | collective-permute-start | bytes 786440 | tf_op jit(solution)/shard_map/ppermute | solution.py:12
  580.2 16.9 %collective-permute-start.13 = (f32[256,64]{0,1:T(8,128)S(1)}, f32[256,64]{0,1:T(8,128)S(1)}, u32[]{:S(2)}, u32[]{:S(2)}) collective-permute-start(f32[256,64]{0,1:T(8,128)S(1)} %fusion.224), channel_id=1, source_target_pairs={{32,0},{36,4},{40,8},{44,12},{48,16},{52,20},{56,24},{60,28},{64,3... | collective-permute-start | bytes 196616 | tf_op jit(solution)/shard_map/ppermute | solution.py:12
  592.7 17.0 %all-to-all-start.4 = ((f32[4,256,64]{1,2,0:T(8,128)}), f32[4,256,64]{1,2,0:T(8,128)S(1)}, u32[]{:S(2)}, u32[]{:S(2)}) async-start(f32[4,256,64]{1,2,0:T(8,128)} %stack.16), calls=%async_computation.4 | async-start | bytes 524288 | tf_op jit(solution)/shard_map/all_to_all | solution.py:104
  674.1 14.1 %collective-permute-start.29 = (f32[16,256]{1,0:T(8,128)S(1)}, f32[16,256]{1,0:T(8,128)S(1)}, u32[]{:S(2)}, u32[]{:S(2)}) collective-permute-start(f32[16,256]{1,0:T(8,128)S(1)} %fusion.222), channel_id=1, source_target_pairs={{64,0},{68,4},{72,8},{76,12},{80,16},{84,20},{88,24},{92,28},{96,3... | collective-permute-start | bytes 49160 | tf_op jit(solution)/shard_map/ppermute | solution.py:12
  678.7 9.8 %collective-permute-start.15 = (f32[256,256]{1,0:T(8,128)S(1)}, f32[256,256]{1,0:T(8,128)S(1)}, u32[]{:S(2)}, u32[]{:S(2)}) collective-permute-start(f32[256,256]{1,0:T(8,128)S(1)} %pad_maximum_fusion.7), channel_id=1, source_target_pairs={{64,0},{68,4},{72,8},{76,12},{80,16},{84,20},{88,24},{92,28},{96,3... | collective-permute-start | bytes 786440 | tf_op jit(solution)/shard_map/ppermute | solution.py:12
  683.1 17.8 %collective-permute-start.16 = (f32[256,64]{0,1:T(8,128)}, f32[256,64]{0,1:T(8,128)}, u32[]{:S(2)}, u32[]{:S(2)}) collective-permute-start(f32[256,64]{0,1:T(8,128)} %fusion.223), channel_id=1, source_target_pairs={{64,0},{68,4},{72,8},{76,12},{80,16},{84,20},{88,24},{92,28},{96,3... | collective-permute-start | bytes 196616 | tf_op jit(solution)/shard_map/ppermute | solution.py:12
  685.6 93.7 %collective-permute-start.28 = (f32[16,256]{1,0:T(8,128)}, f32[16,256]{1,0:T(8,128)S(1)}, u32[]{:S(2)}, u32[]{:S(2)}) collective-permute-start(f32[16,256]{1,0:T(8,128)} %fusion.253), channel_id=1, source_target_pairs={{0,64},{4,68},{8,72},{12,76},{16,80},{20,84},{24,88},{28,92},{32,9... | collective-permute-start | bytes 49160 | tf_op jit(solution)/shard_map/ppermute | solution.py:12
  696.4 17.9 %all-to-all-start.5 = ((f32[4,256,64]{1,2,0:T(8,128)}), f32[4,256,64]{1,2,0:T(8,128)S(1)}, u32[]{:S(2)}, u32[]{:S(2)}) async-start(f32[4,256,64]{1,2,0:T(8,128)} %stack.17), calls=%async_computation.5 | async-start | bytes 524288 | tf_op jit(solution)/shard_map/all_to_all | solution.py:104
  779.6 16.9 %collective-permute-start.31 = (f32[16,256]{1,0:T(8,128)S(1)}, f32[16,256]{1,0:T(8,128)S(1)}, u32[]{:S(2)}, u32[]{:S(2)}) collective-permute-start(f32[16,256]{1,0:T(8,128)S(1)} %fusion.211), channel_id=1, source_target_pairs={{128,0},{132,4},{136,8},{140,12},{144,16},{148,20},{152,24},{156,2... | collective-permute-start | bytes 49160 | tf_op jit(solution)/shard_map/ppermute | solution.py:12
  784.9 11.5 %collective-permute-start.30 = (f32[16,256]{1,0:T(8,128)S(1)}, f32[16,256]{1,0:T(8,128)S(1)}, u32[]{:S(2)}, u32[]{:S(2)}) collective-permute-start(f32[16,256]{1,0:T(8,128)S(1)} %fusion.255), channel_id=1, source_target_pairs={{0,128},{4,132},{8,136},{12,140},{16,144},{20,148},{24,152},{28,15... | collective-permute-start | bytes 49160 | tf_op jit(solution)/shard_map/ppermute | solution.py:12
  786.3 12.3 %collective-permute-start.18 = (f32[256,256]{1,0:T(8,128)S(1)}, f32[256,256]{1,0:T(8,128)S(1)}, u32[]{:S(2)}, u32[]{:S(2)}) collective-permute-start(f32[256,256]{1,0:T(8,128)S(1)} %pad_maximum_fusion.8), channel_id=1, source_target_pairs={{128,0},{132,4},{136,8},{140,12},{144,16},{148,20},{152,24},{156,2... | collective-permute-start | bytes 786440 | tf_op jit(solution)/shard_map/ppermute | solution.py:12
  795.2 10.8 %collective-permute-start.17 = (f32[256,64]{0,1:T(8,128)S(1)}, f32[256,64]{0,1:T(8,128)S(1)}, u32[]{:S(2)}, u32[]{:S(2)}) collective-permute-start(f32[256,64]{0,1:T(8,128)S(1)} %fusion.246), channel_id=1, source_target_pairs={{0,128},{4,132},{8,136},{12,140},{16,144},{20,148},{24,152},{28,15... | collective-permute-start | bytes 196616 | tf_op jit(solution)/shard_map/ppermute | solution.py:12
  (33 other events, 183.9 us)
